TPU v7x, 256 devices: a whole 4x4x8 slice. The times are simulated.
256 devices in a mesh: row: 8 (over z), col: 16 (over y, x), pan: 2 (over core).
Axes of the slice: x: 4, y: 4, z: 8, core: 2. Of those that a mesh axis runs over, the one named last changes fastest.
Arguments:
- plan_values: bfloat16 [8192, 128, 256], P('row', 'col', 'pan'), may hold values from 0.099609375 to 1
- plan_blocks: int32 [8, 128], P('row', 'col'), may hold values from 0 to 127, as said below
- first_values: bfloat16 [32, 3, 256, 256], P('row'), may hold values from -0.21875 to 0.21875
- first_blocks: int32 [32, 3], P('row'), may hold values from 0 to 3, as said below
- second_values: bfloat16 [128, 6, 256, 256], P('col', None, None, 'pan'), may hold values from -0.15625 to 0.15625
- second_blocks: int32 [128, 6], P('col'), may hold values from 0 to 7, as said below
- weight_first: float32 [8192], P('row'), may hold values from 0.5 to 2
- weight_second: float32 [128, 256], P('col', 'pan'), may hold values from 0.5 to 2
- offset_first: float32 [8192], P('row'), may hold values from -3 to 3
- offset_second: float32 [128, 256], P('col', 'pan'), may hold values from -3 to 3
Outputs:
- new_plan: bfloat16 [8192, 128, 256], P('row', 'col', 'pan')
- scale_first: float32 [8192], P('row')
- scale_second: float32 [128, 256], P('col', 'pan')
Inputs may be any that keep to these rules, and one draw needn't show every extreme that they name: `plan_blocks`: each entry is a slice-B block number; its column panel is the entry // 8. Within the 8 slots of one index of col (aligned groups of the second dimension) no column panel is named more than 2 times, and in every row panel one column panel is named exactly 2 times by every such group. `first_blocks`: block numbers within the row panel of the slice-A block; the 3 entries of a row are distinct. `second_blocks`: block numbers within the column panel of the slice-B block; the 6 entries of a row are distinct.
All inputs are finite; a program needn't handle non-finite values.
Results may differ from a plain program's by a relative error of at most 0.0087.
Values may be sent and summed in bfloat16 or wider, within the bound.
No kernel may reach another device: no remote copies, remote signals or barrier semaphores. Data moves between devices by JAX's collectives and lax.ppermute only.
A program may use at most 128 MiB of HBM per device.

v0:
```python
import jax
import jax.numpy as jnp
from jax import lax
from jax.sharding import PartitionSpec as P

CAP = 2


def first_product(plan_values, first_values, first_blocks):
    tile_count = first_blocks.shape[0]
    block_size = first_values.shape[2]
    slot_count = plan_values.shape[1]
    half_width = plan_values.shape[2]
    row_tiles = plan_values.reshape(tile_count, block_size, slot_count * half_width)
    running = jnp.zeros(row_tiles.shape, jnp.float32)
    for neighbor in range(first_blocks.shape[1]):
        picked = jnp.take(row_tiles, first_blocks[:, neighbor], axis=0)
        running = running + jnp.einsum(
            "iab,ibn->ian", first_values[:, neighbor], picked, preferred_element_type=jnp.float32
        )
    return running.astype(jnp.bfloat16).reshape(tile_count * block_size, slot_count, half_width)


def dispatch(chooser, within_panel, product):
    outgoing = jnp.einsum(
        "dcs,rsh->dcrh", chooser.astype(jnp.bfloat16), product, preferred_element_type=jnp.float32
    ).astype(jnp.bfloat16)
    labels = jnp.sum(chooser.astype(jnp.int32) * (within_panel + 1)[None, None, :], axis=2) - 1
    return (outgoing, labels)


def second_product(dense_plan, second_values, second_blocks):
    blocks_here = second_blocks.shape[0]
    columns = jnp.arange(blocks_here)
    placer = (second_blocks[:, :, None] == columns[None, None, :]).astype(jnp.bfloat16)
    panel_matrix = jnp.einsum(
        "kqbh,kql->kblh", second_values, placer, preferred_element_type=jnp.float32
    ).astype(jnp.bfloat16)
    return jnp.einsum("rkb,kblh->rlh", dense_plan, panel_matrix, preferred_element_type=jnp.float32)


def local(
    plan_values,
    plan_blocks,
    first_values,
    first_blocks,
    second_values,
    second_blocks,
    weight_first,
    weight_second,
    offset_first,
    offset_second,
):
    col_count = lax.axis_size("col")
    blocks_here = second_blocks.shape[0]
    slot_count = plan_values.shape[1]
    block_size = first_values.shape[2]
    panel_rows = plan_values.shape[0]
    plan_width = float(slot_count * col_count * block_size)
    named_blocks = plan_blocks[0]
    target_panel = named_blocks // blocks_here
    within_panel = named_blocks % blocks_here
    same_panel = target_panel[:, None] == target_panel[None, :]
    earlier = jnp.arange(slot_count)[:, None] > jnp.arange(slot_count)[None, :]
    position = jnp.sum((same_panel & earlier).astype(jnp.int32), axis=1)
    chooser = (target_panel[None, None, :] == jnp.arange(col_count)[:, None, None]) & (
        position[None, None, :] == jnp.arange(CAP)[None, :, None]
    )
    product = first_product(plan_values, first_values, first_blocks)
    outgoing, labels = dispatch(chooser, within_panel, product)
    incoming, arrival_ids = (
        lax.all_to_all(outgoing, "col", split_axis=0, concat_axis=0, tiled=True),
        lax.all_to_all(labels, "col", split_axis=0, concat_axis=0, tiled=True),
    )
    item_rows = incoming.shape[2]
    arrivals = incoming.reshape(col_count * CAP, item_rows, incoming.shape[3])
    matcher = (arrival_ids.reshape(-1)[:, None] == jnp.arange(blocks_here)[None, :]).astype(
        jnp.bfloat16
    )
    dense_plan = jnp.einsum(
        "ik,irh->rkh", matcher, arrivals, preferred_element_type=jnp.float32
    ).astype(jnp.bfloat16)
    present = jnp.minimum(jnp.sum(matcher.astype(jnp.float32), axis=0), 1.0)
    gathered = lax.all_gather(dense_plan, "pan", axis=2, tiled=True)
    crossed = second_product(gathered, second_values, second_blocks)
    kernel_values = present[None, :, None] * jnp.exp(
        crossed - offset_first[:, None, None] - offset_second[None]
    )
    row_totals = lax.psum(jnp.sum(kernel_values, axis=(1, 2)), ("col", "pan"))
    scale_first = weight_first * plan_width / row_totals
    weighted = kernel_values * scale_first[:, None, None]
    colsum, counts = lax.psum((jnp.sum(weighted, axis=0), present * float(panel_rows)), "row")
    scale_second = weight_second * counts[:, None] / jnp.where(counts[:, None] > 0, colsum, 1.0)
    new_values = (weighted * scale_second[None]).astype(jnp.bfloat16)
    returned = jnp.einsum(
        "ik,rkh->irh", matcher, new_values, preferred_element_type=jnp.float32
    ).astype(jnp.bfloat16)
    returned = returned.reshape(col_count, CAP, item_rows, returned.shape[2])
    homeward = lax.all_to_all(returned, "col", split_axis=0, concat_axis=0, tiled=True)
    new_plan = jnp.einsum(
        "dcs,dcrh->rsh", chooser.astype(jnp.bfloat16), homeward, preferred_element_type=jnp.float32
    ).astype(jnp.bfloat16)
    return (new_plan, scale_first, scale_second)


def solution(mesh):
    return jax.shard_map(
        local,
        mesh=mesh,
        in_specs=(
            P("row", "col", "pan"),
            P("row", "col"),
            P("row", None, None, None),
            P("row", None),
            P("col", None, None, "pan"),
            P("col", None),
            P("row"),
            P("col", "pan"),
            P("row"),
            P("col", "pan"),
        ),
        out_specs=(P("row", "col", "pan"), P("row"), P("col", "pan")),
        check_vma=False,
    )
```

profile of v0, /device:TPU:2, one launch (start us, length us, event | category | flops | bytes accessed | tf_op | source)
XLA Modules:
  0.0 442.7 jit_solution(4532502949180978923)
XLA Ops:
  9.8 7.5 %all-to-all-start = ((s32[16,1,2]{2,1,0:T(1,128)}), s32[16,1,2]{2,1,0:T(1,128)S(1)}, u32[]{:S(2)}, u32[]{:S(2)}) async-start(s32[16,1,2]{2,1,0:T(1,128)} %copy.46), calls=%async_computation | async-start | bytes 16384 | tf_op jit(solution)/shard_map/all_to_all | solution.py:73
  18.4 4.2 reshape.172
  22.6 3.6 gather_fusion.1
  26.1 3.6 gather_fusion.2
  29.7 3.6 gather_fusion
  33.3 2.8 fusion.20
  37.8 2.7 fusion.29
  40.5 4.0 copy.53
  46.7 5.1 %convolution_convert_fusion.1 = bf16[16,2,1024,128]{3,0,2,1:T(8,128)(2,1)} fusion(bf16[1024,8,128,1]{2,1,0,3:T(8,128)(2,1)S(1)} %bitcast.93, pred[2,8]{1,0:T(4,128)(4,1)S(1)} %iota_compare_fusion.4, pred[16,8]{0,1:T(8,128)(4,1)S(1)} %iota_compare_fusion.3), kind=kOutput, calls=%fused_computation.8 | convolution fusion | flops 71303424 | bytes 10485904 | tf_op jit(solution)/shard_map/dcs,rsh->dcrh/dot_general | solution.py:25
  51.8 8.8 %copy.54 = bf16[16,2,1024,128]{3,2,1,0:T(8,128)(2,1)} copy(bf16[16,2,1024,128]{3,0,2,1:T(8,128)(2,1)} %convolution_convert_fusion.1) | data formatting | bytes 16777216 | tf_op jit(solution)/shard_map/convert_element_type | solution.py:27
  60.6 7.2 %all-to-all-start.1 = ((bf16[16,2,1024,128]{3,2,1,0:T(8,128)(2,1)}), bf16[16,2,1024,128]{3,2,1,0:T(8,128)(2,1)}, u32[]{:S(2)}, u32[]{:S(2)}) async-start(bf16[16,2,1024,128]{3,2,1,0:T(8,128)(2,1)} %copy.54), calls=%async_computation.1 | async-start | bytes 16777216 | tf_op jit(solution)/shard_map/all_to_all | solution.py:72
  69.3 118.5 %all-to-all-done.1 = bf16[16,2,1024,128]{3,2,1,0:T(8,128)(2,1)} async-done(((bf16[16,2,1024,128]{3,2,1,0:T(8,128)(2,1)}), bf16[16,2,1024,128]{3,2,1,0:T(8,128)(2,1)}, u32[]{:S(2)}, u32[]{:S(2)}) %all-to-all-start.1) | async-done | bytes 8388640 | tf_op jit(solution)/shard_map/all_to_all | solution.py:72
  187.9 9.3 %convert_bitcast_fusion.1 = bf16[1024,8,128]{2,1,0:T(8,128)(2,1)} fusion(bf16[32,1024,128]{2,1,0:T(8,128)(2,1)} %bitcast.10, s32[32]{0:T(128)S(1)} %eq.91), kind=kOutput, calls=%fused_computation.31 | convolution fusion | flops 68157696 | bytes 10485888 | tf_op jit(solution)/shard_map/ik,irh->rkh/dot_general | solution.py:80
  197.3 4.0 convert_bitcast_fusion
  201.3 18.2 %all-gather.2.cloned.1.call-done = bf16[1024,8,256]{2,1,0:T(8,128)(2,1)} async-done(((bf16[1024,8,128]{2,1,0:T(8,128)(2,1)}), bf16[1024,8,256]{2,1,0:T(8,128)(2,1)}) %all-gather.2.cloned.1.call-update) | async-done | bytes 4194320 | tf_op jit(solution)/shard_map/all_gather | solution.py:84
  219.5 10.1 %fusion.15 = (f32[1024]{0:T(1024)S(1)}, f32[1024,8,128,1]{2,0,3,1:T(8,128)}) fusion(f32[8,128]{1,0:T(8,128)S(1)} %copy-done.7, f32[1024]{0:T(1024)S(1)} %copy-done.8, f32[8]{0:T(128)S(1)} %get-tuple-element.10, bf16[8,256,8,128]{3,2,1,0:T(8,128)(2,1)} %convert_bitcast_fusion, bf16[1024,8,256]{2,1,0:T(8,128)(2,1)} %all-gather.2.cloned.1.call-done), kind=kOutput, calls=%fused_computation.24 | convolution fusion | flops 4299160576 | bytes 12595232 | tf_op jit(solution)/shard_map/rkb,kblh->rlh/dot_general | solution.py:39
  229.6 62.6 %psum.21 = f32[1024]{0:T(1024)S(1)} all-reduce(f32[1024]{0:T(1024)S(1)} %get-tuple-element.13), channel_id=1, replica_groups=mesh['row'=8,'col'=16,'pan'=2] {'col','pan'}, use_global_device_ids=true, to_apply=%region_4.6 | all-reduce | flops 1024 | bytes 8192 | tf_op jit(solution)/shard_map/psum | solution.py:89
  292.2 3.3 multiply_reduce_fusion
  295.5 17.7 %all-reduce = (f32[8,128]{1,0:T(8,128)S(1)}, f32[8]{0:T(128)S(1)}) all-reduce(f32[8,128]{1,0:T(8,128)S(1)} %multiply_reduce_fusion, f32[8]{0:T(128)S(1)} %get-tuple-element.9), channel_id=1, replica_groups=mesh['row'=8,'col'=16,'pan'=2] {'row'}, use_global_device_ids=true, to_apply=%region_7.9 | all-reduce | flops 1032 | bytes 8256 | tf_op jit(solution)/shard_map/psum | solution.py:92
  313.3 3.8 multiply_convert_fusion
  317.2 6.3 %convolution_convert_fusion = bf16[32,1024,128]{2,0,1:T(8,128)(2,1)S(1)} fusion(bf16[1024,8,128]{2,0,1:T(8,128)(2,1)S(1)} %multiply_convert_fusion, s32[32]{0:T(128)S(1)} %eq.91), kind=kOutput, calls=%fused_computation.7 | convolution fusion | flops 71303424 | bytes 10485888 | tf_op jit(solution)/shard_map/ik,rkh->irh/dot_general | solution.py:95
  323.5 8.0 %copy.60 = bf16[16,2,1024,128]{3,1,2,0:T(2,128)(2,1)S(1)} copy(bf16[16,2,1024,128]{3,1,0,2:T(2,128)(2,1)S(1)} %bitcast.91) | data formatting | bytes 16777216 | tf_op jit(solution)/shard_map/reshape | solution.py:98
  331.5 98.3 %all_to_all.16 = bf16[16,2,1024,128]{3,1,2,0:T(2,128)(2,1)S(1)} all-to-all(bf16[16,2,1024,128]{3,1,2,0:T(2,128)(2,1)S(1)} %copy.60), channel_id=1, replica_groups=mesh['row'=8,'col'=16,'pan'=2] {'col'}, dimensions={0} | all-to-all | bytes 16777216 | tf_op jit(solution)/shard_map/all_to_all | solution.py:99
  429.9 6.0 %fusion.32 = bf16[1024,8,128]{2,1,0:T(8,128)(2,1)} fusion(bf16[16,2,1024,128]{3,1,2,0:T(2,128)(2,1)S(1)} %all_to_all.16, pred[2,8]{1,0:T(4,128)(4,1)S(1)} %iota_compare_fusion.4, pred[16,8]{0,1:T(8,128)(4,1)S(1)} %iota_compare_fusion.3), kind=kOutput, calls=%fused_computation.36 | convolution fusion | flops 68157696 | bytes 10485904 | tf_op jit(solution)/shard_map/dcs,dcrh->rsh/dot_general | solution.py:100
  (53 shorter events, 9.3 us)
Async XLA Ops:
  7.2 190.1 %copy-start = (bf16[8,6,256,128]{3,2,1,0:T(8,128)(2,1)S(1)}, bf16[8,6,256,128]{3,2,1,0:T(8,128)(2,1)}, u32[]{:S(2)}) copy-start(bf16[8,6,256,128]{3,2,1,0:T(8,128)(2,1)} %param.16) | copy-start | bytes 9437188
  9.8 50.8 %all-to-all-start = ((s32[16,1,2]{2,1,0:T(1,128)}), s32[16,1,2]{2,1,0:T(1,128)S(1)}, u32[]{:S(2)}, u32[]{:S(2)}) async-start(s32[16,1,2]{2,1,0:T(1,128)} %copy.46), calls=%async_computation | async-start | bytes 16384 | tf_op jit(solution)/shard_map/all_to_all | solution.py:73
  33.3 2.8 copy-start.3
  33.3 2.8 copy-start.4
  36.2 1.6 copy-start.2
  60.6 127.3 %all-to-all-start.1 = ((bf16[16,2,1024,128]{3,2,1,0:T(8,128)(2,1)}), bf16[16,2,1024,128]{3,2,1,0:T(8,128)(2,1)}, u32[]{:S(2)}, u32[]{:S(2)}) async-start(bf16[16,2,1024,128]{3,2,1,0:T(8,128)(2,1)} %copy.54), calls=%async_computation.1 | async-start | bytes 16777216 | tf_op jit(solution)/shard_map/all_to_all | solution.py:72
  67.8 151.7 %all-gather.2.cloned.1.call-start = ((), (), s32[]{:S(2)}) async-start(), calls=%async_computation.3 | async-start | bytes 6291456 | tf_op jit(solution)/shard_map/all_gather | solution.py:84
  187.9 9.4 %copy-start.9 = (s32[8,6]{1,0:T(8,128)S(1)}, s32[8,6]{1,0:T(8,128)}, u32[]{:S(2)}) copy-start(s32[8,6]{1,0:T(8,128)} %param.17) | copy-start | bytes 580
  197.2 22.3 %copy-start.7 = (f32[8,128]{1,0:T(8,128)S(1)}, f32[8,128]{1,0:T(8,128)}, u32[]{:S(2)}) copy-start(f32[8,128]{1,0:T(8,128)} %param.21) | copy-start | bytes 12292
  197.3 22.3 %copy-start.8 = (f32[1024]{0:T(1024)S(1)}, f32[1024]{0:T(1024)}, u32[]{:S(2)}) copy-start(f32[1024]{0:T(1024)} %param.20) | copy-start | bytes 12292
  219.5 72.7 %copy-start.10 = (f32[1024]{0:T(1024)S(1)}, f32[1024]{0:T(1024)}, u32[]{:S(2)}) copy-start(f32[1024]{0:T(1024)} %param.18) | copy-start | bytes 12292
  229.6 83.6 %copy-start.11 = (f32[8,128]{1,0:T(8,128)S(1)}, f32[8,128]{1,0:T(8,128)}, u32[]{:S(2)}) copy-start(f32[8,128]{1,0:T(8,128)} %param.19) | copy-start | bytes 12292
  292.2 24.9 %copy-start.5 = (f32[1024]{0:T(1024)}, f32[1024]{0:T(1024)S(1)}, u32[]{:S(2)}) copy-start(f32[1024]{0:T(1024)S(1)} %multiply_divide_fusion) | copy-start | bytes 12292
  313.3 10.2 %copy-start.6 = (f32[8,128]{1,0:T(8,128)}, f32[8,128]{1,0:T(8,128)S(1)}, u32[]{:S(2)}) copy-start(f32[8,128]{1,0:T(8,128)S(1)} %select_divide_fusion) | copy-start | bytes 12292
  331.5 104.3 %copy-start.1 = (bf16[8,6,256,128]{3,2,1,0:T(8,128)(2,1)S(1)}, bf16[8,6,256,128]{3,2,1,0:T(8,128)(2,1)}, u32[]{:S(2)}) copy-start(bf16[8,6,256,128]{3,2,1,0:T(8,128)(2,1)} %param.16) | copy-start | bytes 9437188
Sparse Core Ops, SparseCore 0:
  197.3 22.1 all-gather.1
where the time goes:
time: 443 us
  blocking collectives  179 us (40%)
  waiting for transfers between devices  137 us (31%)
  matrix products  47.4 us (11%)
  local copies, waits for them, and re-layouts  40.8 us (9%)
  starting transfers between devices  14.9 us (3%)
  between operations  14.3 us (3%)
  other arithmetic  10 us (2%)
    all_to_all x1, waiting for transfers between devices, local(): lax.all_to_all(outgoing, 'col', split_axis=0, concat_axis=0, tiled=True)  119 us
    all_to_all x1, blocking collectives, local(): lax.all_to_all(returned, 'col', split_axis=0, concat_axis=0, tiled=True)  98.3 us
    psum x1, blocking collectives, local(): row_totals = lax.psum(jnp.sum(kernel_values, axis=(1, 2)), ('col', 'pan'))  62.6 us
    all_gather x1, waiting for transfers between devices, local(): gathered = lax.all_gather(dense_plan, 'pan', axis=2, tiled=True)  18.2 us
    psum x1, blocking collectives, local(): lax.psum((jnp.sum(weighted, axis=0), present * float(panel_rows)), 'row')  17.7 us
    gather x3, local copies, waits for them, and re-layouts, first_product(): picked = jnp.take(row_tiles, first_blocks[:, neighbor], axis=0)  10.8 us
    dot_general x1, matrix products, second_product(): jnp.einsum('rkb,kblh->rlh', dense_plan, panel_matrix, preferred_element_t...  10.1 us
    dot_general x1, matrix products, local(): jnp.einsum('ik,irh->rkh', matcher, arrivals, preferred_element_type=jnp.f...  9.33 us
  transfers between devices with their start and end apart: 3, of which 2 were waited for; matrix products, arithmetic and copies ran while one was open for 11% of the time, Pallas kernels for 0%

commit v1 on v0

--- a/solution.py
+++ b/solution.py
@@ -86,7 +86,9 @@
     kernel_values = present[None, :, None] * jnp.exp(
         crossed - offset_first[:, None, None] - offset_second[None]
     )
-    row_totals = lax.psum(jnp.sum(kernel_values, axis=(1, 2)), ("col", "pan"))
+    row_totals = jnp.sum(
+        lax.all_gather(jnp.sum(kernel_values, axis=(1, 2)), ("col", "pan")), axis=0
+    )
     scale_first = weight_first * plan_width / row_totals
     weighted = kernel_values * scale_first[:, None, None]
     colsum, counts = lax.psum((jnp.sum(weighted, axis=0), present * float(panel_rows)), "row")

time: 443 us -> 404 us (0.912)
  blocking collectives: 179 us -> 139 us
    psum x1 -> x0, blocking collectives: 62.6 us -> none  [local(): row_totals = lax.psum(jnp.sum(kernel_values, axis=(1, 2)), ('col', 'pan'))]
    all_gather x0 -> x1, blocking collectives: none -> 24.7 us  [local(): lax.all_gather(jnp.sum(kernel_values, axis=(1, 2)), ('col', 'pan'))]
  transfers between devices with their start and end apart: 3 -> 3, of which waited for: 2 -> 2; matrix products, arithmetic and copies ran while one was open for 11% -> 12% of each run, Pallas kernels for 0% -> 0%
where the time goes in v1:
time: 404 us; the launch traced here: 403 us
  blocking collectives  139 us (34%)
  waiting for transfers between devices  137 us (34%)
  matrix products  47.4 us (12%)
  local copies, waits for them, and re-layouts  40.8 us (10%)
  starting transfers between devices  14.9 us (4%)
  between operations  14.3 us (4%)
  other arithmetic  10 us (2%)
    all_to_all x1, waiting for transfers between devices, local(): lax.all_to_all(outgoing, 'col', split_axis=0, concat_axis=0, tiled=True)  119 us
    all_to_all x1, blocking collectives, local(): lax.all_to_all(returned, 'col', split_axis=0, concat_axis=0, tiled=True)  96.8 us
    all_gather x1, blocking collectives, local(): lax.all_gather(jnp.sum(kernel_values, axis=(1, 2)), ('col', 'pan'))  24.7 us
    all_gather x1, waiting for transfers between devices, local(): gathered = lax.all_gather(dense_plan, 'pan', axis=2, tiled=True)  18.2 us
    psum x1, blocking collectives, local(): lax.psum((jnp.sum(weighted, axis=0), present * float(panel_rows)), 'row')  17.7 us
    gather x3, local copies, waits for them, and re-layouts, first_product(): picked = jnp.take(row_tiles, first_blocks[:, neighbor], axis=0)  10.8 us
    dot_general x1, matrix products, second_product(): jnp.einsum('rkb,kblh->rlh', dense_plan, panel_matrix, preferred_element_t...  10.1 us
    dot_general x1, matrix products, local(): jnp.einsum('ik,irh->rkh', matcher, arrivals, preferred_element_type=jnp.f...  9.33 us
  transfers between devices with their start and end apart: 3, of which 2 were waited for; matrix products, arithmetic and copies ran while one was open for 12% of the time, Pallas kernels for 0%

profile of v1, /device:TPU:2, one launch (start us, length us, event | category | flops | bytes accessed | tf_op | source)
XLA Modules:
  0.0 403.4 jit_solution(6317270987980212334)
XLA Ops:
  9.8 7.5 %all-to-all-start = ((s32[16,1,2]{2,1,0:T(1,128)}), s32[16,1,2]{2,1,0:T(1,128)S(1)}, u32[]{:S(2)}, u32[]{:S(2)}) async-start(s32[16,1,2]{2,1,0:T(1,128)} %copy.46), calls=%async_computation | async-start | bytes 16384 | tf_op jit(solution)/shard_map/all_to_all | solution.py:73
  18.4 4.2 %reshape.172 = bf16[4,256,1024]{2,1,0:T(8,128)(2,1)} reshape(bf16[1024,8,128]{2,1,0:T(8,128)(2,1)} %param.12) | data formatting | bytes 4194304 | tf_op jit(solution)/shard_map/reshape | solution.py:14
  22.6 3.6 gather_fusion.1
  26.1 3.6 gather_fusion.2
  29.7 3.6 gather_fusion
  33.3 2.8 fusion.20
  37.8 2.7 fusion.29
  40.5 4.0 copy.53
  46.7 5.1 %convolution_convert_fusion.1 = bf16[16,2,1024,128]{3,0,2,1:T(8,128)(2,1)} fusion(bf16[1024,8,128,1]{2,1,0,3:T(8,128)(2,1)S(1)} %bitcast.93, pred[2,8]{1,0:T(4,128)(4,1)S(1)} %iota_compare_fusion.4, pred[16,8]{0,1:T(8,128)(4,1)S(1)} %iota_compare_fusion.3), kind=kOutput, calls=%fused_computation.8 | convolution fusion | flops 71303424 | bytes 10485904 | tf_op jit(solution)/shard_map/dcs,rsh->dcrh/dot_general | solution.py:25
  51.8 8.8 %copy.54 = bf16[16,2,1024,128]{3,2,1,0:T(8,128)(2,1)} copy(bf16[16,2,1024,128]{3,0,2,1:T(8,128)(2,1)} %convolution_convert_fusion.1) | data formatting | bytes 16777216 | tf_op jit(solution)/shard_map/convert_element_type | solution.py:27
  60.6 7.2 %all-to-all-start.1 = ((bf16[16,2,1024,128]{3,2,1,0:T(8,128)(2,1)}), bf16[16,2,1024,128]{3,2,1,0:T(8,128)(2,1)}, u32[]{:S(2)}, u32[]{:S(2)}) async-start(bf16[16,2,1024,128]{3,2,1,0:T(8,128)(2,1)} %copy.54), calls=%async_computation.1 | async-start | bytes 16777216 | tf_op jit(solution)/shard_map/all_to_all | solution.py:72
  69.3 118.5 %all-to-all-done.1 = bf16[16,2,1024,128]{3,2,1,0:T(8,128)(2,1)} async-done(((bf16[16,2,1024,128]{3,2,1,0:T(8,128)(2,1)}), bf16[16,2,1024,128]{3,2,1,0:T(8,128)(2,1)}, u32[]{:S(2)}, u32[]{:S(2)}) %all-to-all-start.1) | async-done | bytes 8388640 | tf_op jit(solution)/shard_map/all_to_all | solution.py:72
  187.9 9.3 %convert_bitcast_fusion.1 = bf16[1024,8,128]{2,1,0:T(8,128)(2,1)} fusion(bf16[32,1024,128]{2,1,0:T(8,128)(2,1)} %bitcast.10, s32[32]{0:T(128)S(1)} %eq.91), kind=kOutput, calls=%fused_computation.31 | convolution fusion | flops 68157696 | bytes 10485888 | tf_op jit(solution)/shard_map/ik,irh->rkh/dot_general | solution.py:80
  197.3 4.0 convert_bitcast_fusion
  201.3 18.2 %all-gather.3.cloned.1.call-done = bf16[1024,8,256]{2,1,0:T(8,128)(2,1)} async-done(((bf16[1024,8,128]{2,1,0:T(8,128)(2,1)}), bf16[1024,8,256]{2,1,0:T(8,128)(2,1)}) %all-gather.3.cloned.1.call-update) | async-done | bytes 4194320 | tf_op jit(solution)/shard_map/all_gather | solution.py:84
  219.5 10.1 %fusion.15 = (f32[1024]{0:T(1024)S(1)}, f32[1024,8,128,1]{2,0,3,1:T(8,128)}) fusion(f32[8,128]{1,0:T(8,128)S(1)} %copy-done.7, f32[1024]{0:T(1024)S(1)} %copy-done.8, f32[8]{0:T(128)S(1)} %get-tuple-element.10, bf16[8,256,8,128]{3,2,1,0:T(8,128)(2,1)} %convert_bitcast_fusion, bf16[1024,8,256]{2,1,0:T(8,128)(2,1)} %all-gather.3.cloned.1.call-done), kind=kOutput, calls=%fused_computation.24 | convolution fusion | flops 4299160576 | bytes 12595232 | tf_op jit(solution)/shard_map/rkb,kblh->rlh/dot_general | solution.py:39
  229.6 24.7 %all-gather = f32[32768]{0:T(1024)S(1)} all-gather(f32[1024]{0:T(1024)S(1)} %get-tuple-element.13), channel_id=2, replica_groups=mesh['row'=8,'col'=16,'pan'=2] {'col','pan'}, dimensions={0}, use_global_device_ids=true | all-gather | bytes 135168 | tf_op jit(solution)/shard_map/all_gather | solution.py:90
  254.4 3.3 multiply_reduce_fusion
  257.7 17.7 %all-reduce = (f32[8,128]{1,0:T(8,128)S(1)}, f32[8]{0:T(128)S(1)}) all-reduce(f32[8,128]{1,0:T(8,128)S(1)} %multiply_reduce_fusion, f32[8]{0:T(128)S(1)} %get-tuple-element.9), channel_id=1, replica_groups=mesh['row'=8,'col'=16,'pan'=2] {'row'}, use_global_device_ids=true, to_apply=%region_7.9 | all-reduce | flops 1032 | bytes 8256 | tf_op jit(solution)/shard_map/psum | solution.py:94
  275.5 3.8 multiply_convert_fusion
  279.4 6.3 %convolution_convert_fusion = bf16[32,1024,128]{2,0,1:T(8,128)(2,1)S(1)} fusion(bf16[1024,8,128]{2,0,1:T(8,128)(2,1)S(1)} %multiply_convert_fusion, s32[32]{0:T(128)S(1)} %eq.91), kind=kOutput, calls=%fused_computation.7 | convolution fusion | flops 71303424 | bytes 10485888 | tf_op jit(solution)/shard_map/ik,rkh->irh/dot_general | solution.py:97
  285.7 8.0 %copy.60 = bf16[16,2,1024,128]{3,1,2,0:T(2,128)(2,1)S(1)} copy(bf16[16,2,1024,128]{3,1,0,2:T(2,128)(2,1)S(1)} %bitcast.91) | data formatting | bytes 16777216 | tf_op jit(solution)/shard_map/reshape | solution.py:100
  293.7 96.8 %all_to_all.16 = bf16[16,2,1024,128]{3,1,2,0:T(2,128)(2,1)S(1)} all-to-all(bf16[16,2,1024,128]{3,1,2,0:T(2,128)(2,1)S(1)} %copy.60), channel_id=1, replica_groups=mesh['row'=8,'col'=16,'pan'=2] {'col'}, dimensions={0} | all-to-all | bytes 16777216 | tf_op jit(solution)/shard_map/all_to_all | solution.py:101
  390.5 6.0 %fusion.32 = bf16[1024,8,128]{2,1,0:T(8,128)(2,1)} fusion(bf16[16,2,1024,128]{3,1,2,0:T(2,128)(2,1)S(1)} %all_to_all.16, pred[2,8]{1,0:T(4,128)(4,1)S(1)} %iota_compare_fusion.4, pred[16,8]{0,1:T(8,128)(4,1)S(1)} %iota_compare_fusion.3), kind=kOutput, calls=%fused_computation.36 | convolution fusion | flops 68157696 | bytes 10485904 | tf_op jit(solution)/shard_map/dcs,dcrh->rsh/dot_general | solution.py:102
  (55 shorter events, 9.3 us)
Async XLA Ops:
  7.2 190.1 %copy-start = (bf16[8,6,256,128]{3,2,1,0:T(8,128)(2,1)S(1)}, bf16[8,6,256,128]{3,2,1,0:T(8,128)(2,1)}, u32[]{:S(2)}) copy-start(bf16[8,6,256,128]{3,2,1,0:T(8,128)(2,1)} %param.16) | copy-start | bytes 9437188
  9.8 50.8 %all-to-all-start = ((s32[16,1,2]{2,1,0:T(1,128)}), s32[16,1,2]{2,1,0:T(1,128)S(1)}, u32[]{:S(2)}, u32[]{:S(2)}) async-start(s32[16,1,2]{2,1,0:T(1,128)} %copy.46), calls=%async_computation | async-start | bytes 16384 | tf_op jit(solution)/shard_map/all_to_all | solution.py:73
  33.3 2.8 copy-start.3
  33.3 2.8 copy-start.4
  36.2 1.6 copy-start.2
  60.6 127.3 %all-to-all-start.1 = ((bf16[16,2,1024,128]{3,2,1,0:T(8,128)(2,1)}), bf16[16,2,1024,128]{3,2,1,0:T(8,128)(2,1)}, u32[]{:S(2)}, u32[]{:S(2)}) async-start(bf16[16,2,1024,128]{3,2,1,0:T(8,128)(2,1)} %copy.54), calls=%async_computation.1 | async-start | bytes 16777216 | tf_op jit(solution)/shard_map/all_to_all | solution.py:72
  67.8 151.7 %all-gather.3.cloned.1.call-start = ((), (), s32[]{:S(2)}) async-start(), calls=%async_computation.3 | async-start | bytes 6291456 | tf_op jit(solution)/shard_map/all_gather | solution.py:84
  187.9 9.4 %copy-start.9 = (s32[8,6]{1,0:T(8,128)S(1)}, s32[8,6]{1,0:T(8,128)}, u32[]{:S(2)}) copy-start(s32[8,6]{1,0:T(8,128)} %param.17) | copy-start | bytes 580
  197.2 22.3 %copy-start.7 = (f32[8,128]{1,0:T(8,128)S(1)}, f32[8,128]{1,0:T(8,128)}, u32[]{:S(2)}) copy-start(f32[8,128]{1,0:T(8,128)} %param.21) | copy-start | bytes 12292
  197.3 22.3 %copy-start.8 = (f32[1024]{0:T(1024)S(1)}, f32[1024]{0:T(1024)}, u32[]{:S(2)}) copy-start(f32[1024]{0:T(1024)} %param.20) | copy-start | bytes 12292
  219.5 34.9 %copy-start.10 = (f32[1024]{0:T(1024)S(1)}, f32[1024]{0:T(1024)}, u32[]{:S(2)}) copy-start(f32[1024]{0:T(1024)} %param.18) | copy-start | bytes 12292
  229.6 45.8 %copy-start.11 = (f32[8,128]{1,0:T(8,128)S(1)}, f32[8,128]{1,0:T(8,128)}, u32[]{:S(2)}) copy-start(f32[8,128]{1,0:T(8,128)} %param.19) | copy-start | bytes 12292
  254.4 25.0 %copy-start.5 = (f32[1024]{0:T(1024)}, f32[1024]{0:T(1024)S(1)}, u32[]{:S(2)}) copy-start(f32[1024]{0:T(1024)S(1)} %multiply_divide_fusion) | copy-start | bytes 12292
  275.5 10.2 %copy-start.6 = (f32[8,128]{1,0:T(8,128)}, f32[8,128]{1,0:T(8,128)S(1)}, u32[]{:S(2)}) copy-start(f32[8,128]{1,0:T(8,128)S(1)} %select_divide_fusion) | copy-start | bytes 12292
  293.7 102.8 %copy-start.1 = (bf16[8,6,256,128]{3,2,1,0:T(8,128)(2,1)S(1)}, bf16[8,6,256,128]{3,2,1,0:T(8,128)(2,1)}, u32[]{:S(2)}) copy-start(bf16[8,6,256,128]{3,2,1,0:T(8,128)(2,1)} %param.16) | copy-start | bytes 9437188
Sparse Core Ops, SparseCore 0:
  197.3 22.1 all-gather.2
